TPU v7x, 32 devices: a whole 2x2x4 slice. The times are simulated.
32 devices in a mesh: energy: 8 (over y, x, core), space: 4 (over z).
Axes of the slice: x: 2, y: 2, z: 4, core: 2. Of those that a mesh axis runs over, the one named last changes fastest.
Arguments:
- screening: bfloat16 [8, 8, 3, 2, 128, 128], P('energy', 'space'), may hold values from -0.21875 to 0.21875
- polarization: bfloat16 [8, 8, 3, 2, 128, 128], P('energy', 'space'), may hold values from -6 to 6
- propagator: bfloat16 [8, 8, 3, 2, 128, 128], P('energy', 'space'), may hold values from -0.21875 to 0.21875
Outputs:
- dressed: bfloat16 [8, 8, 3, 2, 128, 128], P('energy', 'space')
All inputs are finite; a program needn't handle non-finite values.
Results may differ from a plain program's by a relative error of at most 0.015.
Values may be sent and summed in bfloat16 or wider, within the bound.
No kernel may reach another device: no remote copies, remote signals or barrier semaphores. Data moves between devices by JAX's collectives and lax.ppermute only.
A program may use at most 64 MiB of HBM per device.

v0:
```python
import math
import jax
import jax.numpy as jnp
from jax import lax
from jax.sharding import PartitionSpec as P


def with_halo(x, sides, width):
    for axis, dim in sides:
        peers, length = (lax.axis_size(axis), x.shape[dim])
        up = [(i, (i + 1) % peers) for i in range(peers - 1)]
        down = [(j, i) for i, j in up]
        last = lax.slice_in_dim(x, length - width, length, axis=dim)
        leading = lax.slice_in_dim(x, 0, width, axis=dim)
        before = lax.ppermute(last, axis, up)
        after = lax.ppermute(leading, axis, down)
        x = jnp.concatenate([before, x, after], axis=dim)
    return x


def clip_edges(banded, first_row, row_total):
    row_count = banded.shape[1]
    row_index = first_row + jnp.arange(row_count, dtype=jnp.int32)
    band_index = jnp.arange(3, dtype=jnp.int32)
    dropped = (band_index[None, :] == 0) & (row_index[:, None] == 0) | (
        band_index[None, :] == 2
    ) & (row_index[:, None] == row_total - 1)
    keep_mask = jnp.where(dropped, 0.0, 1.0).astype(banded.dtype)
    return banded * keep_mask[None, :, :, None, None, None]


def complex_product(first, second, adjoint):
    first_real = first[:, :, 0]
    first_imag = first[:, :, 1]
    second_real = second[:, :, 0]
    second_imag = second[:, :, 1]
    if adjoint:
        form = "erij,erkj->erik"
    else:
        form = "erij,erjk->erik"

    def product(lhs, rhs):
        return jnp.einsum(form, lhs, rhs, preferred_element_type=jnp.float32)

    if adjoint:
        real_part = product(first_real, second_real) + product(first_imag, second_imag)
        imag_part = product(first_imag, second_real) - product(first_real, second_imag)
    else:
        real_part = product(first_real, second_real) - product(first_imag, second_imag)
        imag_part = product(first_real, second_imag) + product(first_imag, second_real)
    return jnp.stack([real_part, imag_part], axis=2)


def pick_rows(banded, start, row_count, band):
    return lax.slice_in_dim(banded, start, start + row_count, axis=1)[:, :, band]


def sandwich(outside, between):
    row_count = outside.shape[1] - 2
    products = {}
    for offset in range(-2, 3):
        summed = None
        for inner in range(-1, 2):
            if abs(offset - inner) <= 1:
                term = complex_product(
                    pick_rows(outside, 1, row_count, inner + 1),
                    pick_rows(between, 1 + inner, row_count, offset - inner + 1),
                    False,
                )
                summed = term if summed is None else summed + term
        products[offset] = summed.astype(jnp.bfloat16)
    bands = []
    for target in range(-1, 2):
        summed = None
        for offset in range(target - 1, target + 2):
            term = complex_product(
                products[offset],
                pick_rows(outside, 1 + target, row_count, offset - target + 1),
                True,
            )
            summed = term if summed is None else summed + term
        bands.append(summed)
    return jnp.stack(bands, axis=2)


def split_table(table):
    upper = table.astype(jnp.bfloat16)
    lower = (table - upper.astype(jnp.float32)).astype(jnp.bfloat16)
    return (upper, lower)


def plain_dot(lhs, rhs):
    return jnp.dot(lhs, rhs, preferred_element_type=jnp.float32)


def table_times_data(table_pair, data):
    return plain_dot(table_pair[0], data) + plain_dot(table_pair[1], data)


def table_times_float(table_pair, values):
    value_upper, value_lower = split_table(values)
    return (
        plain_dot(table_pair[0], value_upper)
        + plain_dot(table_pair[0], value_lower)
        + plain_dot(table_pair[1], value_upper)
    )


def convolve(propa_owned, screen_owned, factor):
    energy_count = propa_owned.shape[0]
    owned_shape = propa_owned[:, :, :, 0].shape
    freq_index = jnp.arange(2 * energy_count, dtype=jnp.int32)
    time_index = jnp.arange(energy_count, dtype=jnp.int32)
    phase = freq_index[:, None] * time_index[None, :] % (2 * energy_count)
    angle = phase.astype(jnp.float32) * (math.pi / energy_count)
    cosine = jnp.cos(angle)
    sine = jnp.sin(angle)
    cos_fwd = split_table(cosine)
    sin_fwd = split_table(sine)
    cos_back = split_table(cosine.T)
    sin_back = split_table(sine.T)

    def forward(banded):
        real_part = banded[:, :, :, 0].reshape(energy_count, -1)
        imag_part = banded[:, :, :, 1].reshape(energy_count, -1)
        return (
            table_times_data(cos_fwd, real_part) + table_times_data(sin_fwd, imag_part),
            table_times_data(cos_fwd, imag_part) - table_times_data(sin_fwd, real_part),
        )

    propa_real, propa_imag = forward(propa_owned)
    screen_real, screen_imag = forward(screen_owned)
    spec_real = propa_real * screen_real - propa_imag * screen_imag
    spec_imag = propa_real * screen_imag + propa_imag * screen_real
    weight = factor / (2 * energy_count)
    out_real = (
        table_times_float(cos_back, spec_real) - table_times_float(sin_back, spec_imag)
    ) * weight
    out_imag = (
        table_times_float(cos_back, spec_imag) + table_times_float(sin_back, spec_real)
    ) * weight
    return jnp.stack([out_real.reshape(owned_shape), out_imag.reshape(owned_shape)], axis=3)


def local(screening, polarization, propagator):
    row_count = screening.shape[1]
    order = screening.shape[-1]
    first_row = lax.axis_index("space") * row_count
    row_total = lax.axis_size("space") * row_count
    screen_masked = clip_edges(screening, first_row, row_total)
    polar_masked = clip_edges(polarization, first_row, row_total)
    propa_masked = clip_edges(propagator, first_row, row_total)
    rimmed = with_halo(jnp.stack([screen_masked, polar_masked, propa_masked]), (("space", 2),), 1)
    screen_padded = rimmed[0]
    polar_padded = rimmed[1]
    propa_padded = rimmed[2]
    screened = sandwich(screen_padded, polar_padded).astype(jnp.bfloat16)
    screen_owned, propa_owned = (
        lax.all_to_all(screened, "energy", split_axis=4, concat_axis=0, tiled=True),
        lax.all_to_all(propa_masked, "energy", split_axis=4, concat_axis=0, tiled=True),
    )
    energy_count = screen_owned.shape[0]
    factor = (3.0 * order / energy_count) ** 0.5
    sigma_owned = convolve(propa_owned, screen_owned, factor).astype(jnp.bfloat16)
    sigma = lax.all_to_all(sigma_owned, "energy", split_axis=0, concat_axis=4, tiled=True)
    sigma_padded = with_halo(sigma, (("space", 1),), 1)
    return sandwich(propa_padded, sigma_padded).astype(jnp.bfloat16)


def solution(mesh):
    in_specs = (
        P("energy", "space", None, None, None, None),
        P("energy", "space", None, None, None, None),
        P("energy", "space", None, None, None, None),
    )
    out_specs = P("energy", "space", None, None, None, None)
    return jax.shard_map(local, mesh=mesh, in_specs=in_specs, out_specs=out_specs, check_vma=False)
```

profile of v0, /device:TPU:0, one launch (start us, length us, event | category | flops | bytes accessed | tf_op | source)
XLA Modules:
  0.0 100.8 jit_solution(13113473520460223739)
XLA Ops:
  0.1 1.4 %fusion.83 = (bf16[1,1,2,3,2,128,128]{6,5,2,4,3,1,0:T(8,128)(2,1)S(1)}, bf16[1,1,2,3,2,128,128]{6,5,2,4,3,1,0:T(8,128)(2,1)S(1)}, bf16[1,2,3,2,128,128]{5,4,1,3,2,0:T(8,128)(2,1)S(1)}) fusion(bf16[1,2,3,2,128,128]{5,4,3,2,1,0:T(8,128)(2,1)} %param.3, bf16[2,3]{0,1:T(4,128)(2,1)S(1)} %select_convert_fusion, bf16[1,2,3,2,128,128]{5,4,3,2,1,0:T(8,128)(2,1)} %param.4, ...), kind=kLoop, calls=%fused_computation.188 | loop fusion | flops 589824 | bytes 2359308 | tf_op jit(solution)/shard_map/stack | solution.py:153
  1.5 1.2 %copy.19 = bf16[1,2,3,2,128,128]{5,1,3,2,0,4:T(2,128)(2,1)} copy(bf16[1,2,3,2,128,128]{5,4,1,3,2,0:T(8,128)(2,1)S(1)} %get-tuple-element.59) | data formatting | bytes 786432 | tf_op jit(solution)/shard_map/mul | solution.py:29
  2.6 5.2 %all-to-all-start = ((bf16[1,2,3,2,128,128]{5,1,3,2,0,4:T(2,128)(2,1)}), bf16[1,2,3,2,128,128]{5,1,3,2,0,4:T(2,128)(2,1)S(1)}, u32[]{:S(2)}, u32[]{:S(2)}) async-start(bf16[1,2,3,2,128,128]{5,1,3,2,0,4:T(2,128)(2,1)} %copy.19), calls=%async_computation | async-start | bytes 786432 | tf_op jit(solution)/shard_map/all_to_all | solution.py:160
  8.0 1.2 %fusion.358 = (bf16[3,1,1,3,2,128,128]{6,5,2,4,3,1,0:T(8,128)(2,1)}, bf16[3,1,1,3,2,128,128]{6,5,2,4,3,1,0:T(8,128)(2,1)}) fusion(bf16[3,1,2,3,2,128,128]{6,5,2,4,3,1,0:T(8,128)(2,1)S(1)} %pad_maximum_fusion.1), kind=kLoop, calls=%fused_computation.593 | loop fusion | bytes 2359296 | tf_op jit(solution)/shard_map/slice | solution.py:13
  9.1 4.3 %collective-permute-start = (bf16[3,1,1,3,2,128,128]{6,5,2,4,3,1,0:T(8,128)(2,1)}, bf16[3,1,1,3,2,128,128]{6,5,2,4,3,1,0:T(8,128)(2,1)}, u32[]{:S(2)}, u32[]{:S(2)}) collective-permute-start(bf16[3,1,1,3,2,128,128]{6,5,2,4,3,1,0:T(8,128)(2,1)} %get-tuple-element.10), channel_id=1, source_target_pairs={{0,1},{1,2},{2,3},{4,5},{5,6},{6,7},{8,9},{9,10},{10,11},{12,13},{... | collective-permute-start | bytes 1769480 | tf_op jit(solution)/shard_map/ppermute | solution.py:15
  13.4 1.3 %collective-permute-start.1 = (bf16[3,1,1,3,2,128,128]{6,5,2,4,3,1,0:T(8,128)(2,1)}, bf16[3,1,1,3,2,128,128]{6,5,2,4,3,1,0:T(8,128)(2,1)}, u32[]{:S(2)}, u32[]{:S(2)}) collective-permute-start(bf16[3,1,1,3,2,128,128]{6,5,2,4,3,1,0:T(8,128)(2,1)} %get-tuple-element.11), channel_id=1, source_target_pairs={{1,0},{2,1},{3,2},{5,4},{6,5},{7,6},{9,8},{10,9},{11,10},{13,12},{... | collective-permute-start | bytes 1769480 | tf_op jit(solution)/shard_map/ppermute | solution.py:16
  14.7 1.4 %all-to-all-done = bf16[1,2,3,2,128,128]{5,1,3,2,0,4:T(2,128)(2,1)S(1)} async-done(((bf16[1,2,3,2,128,128]{5,1,3,2,0,4:T(2,128)(2,1)}), bf16[1,2,3,2,128,128]{5,1,3,2,0,4:T(2,128)(2,1)S(1)}, u32[]{:S(2)}, u32[]{:S(2)}) %all-to-all-start) | async-done | bytes 393248 | tf_op jit(solution)/shard_map/all_to_all | solution.py:160
  16.3 1.2 %fusion.203 = f32[16,12288]{1,0:T(8,128)} fusion(bf16[8,12288]{1,0:T(8,128)(2,1)S(1)} %reshape_squeeze.13), kind=kOutput, calls=%fused_computation.447 | convolution fusion | flops 3147648 | bytes 983040 | tf_op jit(solution)/shard_map/dot_general | solution.py:93
  17.9 0.3 fusion.211
  18.2 0.3 convolution_add_fusion.7
  18.5 1.2 %convolution_add_fusion.3 = f32[16,12288]{1,0:T(8,128)} fusion(f32[16,12288]{1,0:T(8,128)S(1)} %fusion.207, bf16[8,12288]{1,0:T(8,128)(2,1)S(1)} %reshape_squeeze.13), kind=kOutput, calls=%fused_computation.5 | convolution fusion | flops 3344640 | bytes 1769472 | tf_op jit(solution)/shard_map/dot_general | solution.py:93
  19.7 6.4 %collective-permute-done = bf16[3,1,1,3,2,128,128]{6,5,2,4,3,1,0:T(8,128)(2,1)} collective-permute-done((bf16[3,1,1,3,2,128,128]{6,5,2,4,3,1,0:T(8,128)(2,1)}, bf16[3,1,1,3,2,128,128]{6,5,2,4,3,1,0:T(8,128)(2,1)}, u32[]{:S(2)}, u32[]{:S(2)}) %collective-permute-start) | collective-permute-done | bytes 589856 | tf_op jit(solution)/shard_map/ppermute | solution.py:15
  26.2 4.9 %collective-permute-done.1 = bf16[3,1,1,3,2,128,128]{6,5,2,4,3,1,0:T(8,128)(2,1)} collective-permute-done((bf16[3,1,1,3,2,128,128]{6,5,2,4,3,1,0:T(8,128)(2,1)}, bf16[3,1,1,3,2,128,128]{6,5,2,4,3,1,0:T(8,128)(2,1)}, u32[]{:S(2)}, u32[]{:S(2)}) %collective-permute-start.1) | collective-permute-done | bytes 589856 | tf_op jit(solution)/shard_map/ppermute | solution.py:16
  31.1 1.4 %pad_maximum_fusion = bf16[3,1,4,3,2,128,128]{6,5,2,4,3,1,0:T(8,128)(2,1)S(1)} fusion(bf16[3,1,1,3,2,128,128]{6,5,2,4,3,1,0:T(8,128)(2,1)} %collective-permute-done.1, bf16[1,1,2,3,2,128,128]{6,5,2,4,3,1,0:T(8,128)(2,1)S(1)} %bitcast.730, bf16[1,1,2,3,2,128,128]{6,5,2,4,3,1,0:T(8,128)(2,1)S(1)} %get-tuple-element.58, ...), kind=kLoop, calls=%fused_computation.26 | loop fusion | flops 4718592 | bytes 4718592 | tf_op jit(solution)/shard_map/concatenate | solution.py:17
  45.6 1.2 %copy.21 = bf16[1,2,3,2,128,128]{5,1,3,2,0,4:T(2,128)(2,1)} copy(bf16[1,2,3,2,128,128]{5,4,1,3,2,0:T(8,128)(2,1)S(1)} %pad_maximum_fusion.2) | data formatting | bytes 786432 | tf_op jit(solution)/shard_map/stack | solution.py:83
  46.7 3.8 %all-to-all-start.1 = ((bf16[1,2,3,2,128,128]{5,1,3,2,0,4:T(2,128)(2,1)}), bf16[1,2,3,2,128,128]{5,1,3,2,0,4:T(2,128)(2,1)S(1)}, u32[]{:S(2)}, u32[]{:S(2)}) async-start(bf16[1,2,3,2,128,128]{5,1,3,2,0,4:T(2,128)(2,1)} %copy.21), calls=%async_computation.1 | async-start | bytes 786432 | tf_op jit(solution)/shard_map/all_to_all | solution.py:159
  50.6 1.2 %fusion.199 = f32[16,12288]{1,0:T(8,128)} fusion(bf16[8,12288]{1,0:T(8,128)(2,1)S(1)} %reshape_squeeze.12), kind=kOutput, calls=%fused_computation.445 | convolution fusion | flops 3147648 | bytes 983040 | tf_op jit(solution)/shard_map/dot_general | solution.py:93
  51.8 1.2 %fusion.3 = f32[16,12288]{1,0:T(8,128)} fusion(f32[16,12288]{1,0:T(8,128)S(1)} %convolution_add_fusion.7, f32[16,12288]{1,0:T(8,128)S(1)} %copy-done.1, bf16[8,12288]{1,0:T(8,128)(2,1)S(1)} %reshape_squeeze.13), kind=kOutput, calls=%fused_computation.10 | convolution fusion | flops 3541248 | bytes 2555904 | tf_op jit(solution)/shard_map/dot_general | solution.py:93
  53.0 5.9 %all-to-all-done.1 = bf16[1,2,3,2,128,128]{5,1,3,2,0,4:T(2,128)(2,1)S(1)} async-done(((bf16[1,2,3,2,128,128]{5,1,3,2,0,4:T(2,128)(2,1)}), bf16[1,2,3,2,128,128]{5,1,3,2,0,4:T(2,128)(2,1)S(1)}, u32[]{:S(2)}, u32[]{:S(2)}) %all-to-all-start.1) | async-done | bytes 393248 | tf_op jit(solution)/shard_map/all_to_all | solution.py:159
  59.1 0.3 fusion.201
  60.4 0.3 convolution_add_fusion.5
  60.7 0.3 convolution_add_fusion.1
  61.0 0.3 fusion.2
  61.3 0.3 fusion
  61.6 0.5 copy-done
  62.6 0.4 multiply_subtract_fusion
  66.1 10.7 %all_to_all.54 = bf16[8,2,3,2,16,128]{5,4,2,1,3,0:T(8,128)(2,1)S(1)} all-to-all(bf16[8,2,3,2,16,128]{5,4,2,1,3,0:T(8,128)(2,1)S(1)} %pad_maximum_fusion.3), channel_id=1, replica_groups=mesh['energy'=8,'space'=4] {'energy'}, dimensions={0} | all-to-all | bytes 786432 | tf_op jit(solution)/shard_map/all_to_all | solution.py:165
  76.8 2.7 %collective-permute-start.2 = (bf16[1,1,3,2,128,128]{5,4,1,3,2,0:T(8,128)(2,1)S(1)}, bf16[1,1,3,2,128,128]{5,4,1,3,2,0:T(8,128)(2,1)S(1)}, u32[]{:S(2)}, u32[]{:S(2)}) collective-permute-start(bf16[1,1,3,2,128,128]{5,4,1,3,2,0:T(8,128)(2,1)S(1)} %get-tuple-element.51), channel_id=1, source_target_pairs={{0,1},{1,2},{2,3},{4,5},{5,6},{6,7},{8,9},{9,10},{10,11},{12,13},{... | collective-permute-start | bytes 589832 | tf_op jit(solution)/shard_map/ppermute | solution.py:15
  79.6 1.3 %collective-permute-start.3 = (bf16[1,1,3,2,128,128]{5,4,1,3,2,0:T(8,128)(2,1)S(1)}, bf16[1,1,3,2,128,128]{5,4,1,3,2,0:T(8,128)(2,1)S(1)}, u32[]{:S(2)}, u32[]{:S(2)}) collective-permute-start(bf16[1,1,3,2,128,128]{5,4,1,3,2,0:T(8,128)(2,1)S(1)} %get-tuple-element.52), channel_id=1, source_target_pairs={{1,0},{2,1},{3,2},{5,4},{6,5},{7,6},{9,8},{10,9},{11,10},{13,12},{... | collective-permute-start | bytes 589832 | tf_op jit(solution)/shard_map/ppermute | solution.py:16
  81.1 2.3 %collective-permute-done.2 = bf16[1,1,3,2,128,128]{5,4,1,3,2,0:T(8,128)(2,1)S(1)} collective-permute-done((bf16[1,1,3,2,128,128]{5,4,1,3,2,0:T(8,128)(2,1)S(1)}, bf16[1,1,3,2,128,128]{5,4,1,3,2,0:T(8,128)(2,1)S(1)}, u32[]{:S(2)}, u32[]{:S(2)}) %collective-permute-start.2) | collective-permute-done | bytes 196640 | tf_op jit(solution)/shard_map/ppermute | solution.py:15
  83.4 4.1 %collective-permute-done.3 = bf16[1,1,3,2,128,128]{5,4,1,3,2,0:T(8,128)(2,1)S(1)} collective-permute-done((bf16[1,1,3,2,128,128]{5,4,1,3,2,0:T(8,128)(2,1)S(1)}, bf16[1,1,3,2,128,128]{5,4,1,3,2,0:T(8,128)(2,1)S(1)}, u32[]{:S(2)}, u32[]{:S(2)}) %collective-permute-start.3) | collective-permute-done | bytes 196640 | tf_op jit(solution)/shard_map/ppermute | solution.py:16
  100.0 0.8 copy.26
  (203 shorter events, 30.9 us)
Async XLA Ops:
  2.6 13.5 %all-to-all-start = ((bf16[1,2,3,2,128,128]{5,1,3,2,0,4:T(2,128)(2,1)}), bf16[1,2,3,2,128,128]{5,1,3,2,0,4:T(2,128)(2,1)S(1)}, u32[]{:S(2)}, u32[]{:S(2)}) async-start(bf16[1,2,3,2,128,128]{5,1,3,2,0,4:T(2,128)(2,1)} %copy.19), calls=%async_computation | async-start | bytes 786432 | tf_op jit(solution)/shard_map/all_to_all | solution.py:160
  9.1 17.0 %collective-permute-start = (bf16[3,1,1,3,2,128,128]{6,5,2,4,3,1,0:T(8,128)(2,1)}, bf16[3,1,1,3,2,128,128]{6,5,2,4,3,1,0:T(8,128)(2,1)}, u32[]{:S(2)}, u32[]{:S(2)}) collective-permute-start(bf16[3,1,1,3,2,128,128]{6,5,2,4,3,1,0:T(8,128)(2,1)} %get-tuple-element.10), channel_id=1, source_target_pairs={{0,1},{1,2},{2,3},{4,5},{5,6},{6,7},{8,9},{9,10},{10,11},{12,13},{... | collective-permute-start | bytes 1769480 | tf_op jit(solution)/shard_map/ppermute | solution.py:15
  13.4 17.7 %collective-permute-start.1 = (bf16[3,1,1,3,2,128,128]{6,5,2,4,3,1,0:T(8,128)(2,1)}, bf16[3,1,1,3,2,128,128]{6,5,2,4,3,1,0:T(8,128)(2,1)}, u32[]{:S(2)}, u32[]{:S(2)}) collective-permute-start(bf16[3,1,1,3,2,128,128]{6,5,2,4,3,1,0:T(8,128)(2,1)} %get-tuple-element.11), channel_id=1, source_target_pairs={{1,0},{2,1},{3,2},{5,4},{6,5},{7,6},{9,8},{10,9},{11,10},{13,12},{... | collective-permute-start | bytes 1769480 | tf_op jit(solution)/shard_map/ppermute | solution.py:16
  45.4 6.3 %copy-start.1 = (f32[16,12288]{1,0:T(8,128)S(1)}, f32[16,12288]{1,0:T(8,128)}, u32[]{:S(2)}) copy-start(f32[16,12288]{1,0:T(8,128)} %fusion.203) | copy-start | bytes 2359300
  46.7 12.1 %all-to-all-start.1 = ((bf16[1,2,3,2,128,128]{5,1,3,2,0,4:T(2,128)(2,1)}), bf16[1,2,3,2,128,128]{5,1,3,2,0,4:T(2,128)(2,1)S(1)}, u32[]{:S(2)}, u32[]{:S(2)}) async-start(bf16[1,2,3,2,128,128]{5,1,3,2,0,4:T(2,128)(2,1)} %copy.21), calls=%async_computation.1 | async-start | bytes 786432 | tf_op jit(solution)/shard_map/all_to_all | solution.py:159
  61.0 1.1 %copy-start = (f32[16,12288]{1,0:T(8,128)S(1)}, f32[16,12288]{1,0:T(8,128)}, u32[]{:S(2)}) copy-start(f32[16,12288]{1,0:T(8,128)} %convolution_add_fusion.3) | copy-start | bytes 2359300
  61.0 1.4 %copy-start.2 = (f32[16,12288]{1,0:T(8,128)S(1)}, f32[16,12288]{1,0:T(8,128)}, u32[]{:S(2)}) copy-start(f32[16,12288]{1,0:T(8,128)} %fusion.199) | copy-start | bytes 2359300
  61.0 1.6 %copy-start.3 = (f32[16,12288]{1,0:T(8,128)S(1)}, f32[16,12288]{1,0:T(8,128)}, u32[]{:S(2)}) copy-start(f32[16,12288]{1,0:T(8,128)} %fusion.3) | copy-start | bytes 2359300
  76.8 6.5 %collective-permute-start.2 = (bf16[1,1,3,2,128,128]{5,4,1,3,2,0:T(8,128)(2,1)S(1)}, bf16[1,1,3,2,128,128]{5,4,1,3,2,0:T(8,128)(2,1)S(1)}, u32[]{:S(2)}, u32[]{:S(2)}) collective-permute-start(bf16[1,1,3,2,128,128]{5,4,1,3,2,0:T(8,128)(2,1)S(1)} %get-tuple-element.51), channel_id=1, source_target_pairs={{0,1},{1,2},{2,3},{4,5},{5,6},{6,7},{8,9},{9,10},{10,11},{12,13},{... | collective-permute-start | bytes 589832 | tf_op jit(solution)/shard_map/ppermute | solution.py:15
  79.6 8.0 %collective-permute-start.3 = (bf16[1,1,3,2,128,128]{5,4,1,3,2,0:T(8,128)(2,1)S(1)}, bf16[1,1,3,2,128,128]{5,4,1,3,2,0:T(8,128)(2,1)S(1)}, u32[]{:S(2)}, u32[]{:S(2)}) collective-permute-start(bf16[1,1,3,2,128,128]{5,4,1,3,2,0:T(8,128)(2,1)S(1)} %get-tuple-element.52), channel_id=1, source_target_pairs={{1,0},{2,1},{3,2},{5,4},{6,5},{7,6},{9,8},{10,9},{11,10},{13,12},{... | collective-permute-start | bytes 589832 | tf_op jit(solution)/shard_map/ppermute | solution.py:16
where the time goes:
time: 101 us
  matrix products  35.2 us (35%)
  waiting for transfers between devices  25.1 us (25%)
  starting transfers between devices  18.6 us (18%)
  blocking collectives  10.7 us (11%)
  local copies, waits for them, and re-layouts  6.76 us (7%)
  other arithmetic  3.78 us (4%)
    dot_general x144, matrix products, product(): return jnp.einsum(form, lhs, rhs, preferred_element_type=jnp.float32)  23.9 us
    dot_general x28, matrix products, plain_dot(): return jnp.dot(lhs, rhs, preferred_element_type=jnp.float32)  11.4 us
    all_to_all x1, blocking collectives, local(): lax.all_to_all(sigma_owned, 'energy', split_axis=0, concat_axis=4, tiled=...  10.7 us
    ppermute x2, waiting for transfers between devices, with_halo(): after = lax.ppermute(leading, axis, down)  9.03 us
    ppermute x2, waiting for transfers between devices, with_halo(): before = lax.ppermute(last, axis, up)  8.72 us
    ppermute x2, starting transfers between devices, with_halo(): before = lax.ppermute(last, axis, up)  6.99 us
    all_to_all x1, waiting for transfers between devices, local(): lax.all_to_all(screened, 'energy', split_axis=4, concat_axis=0, tiled=True)  5.9 us
    all_to_all x1, starting transfers between devices, local(): lax.all_to_all(propa_masked, 'energy', split_axis=4, concat_axis=0, tiled...  5.2 us
  transfers between devices with their start and end apart: 6, of which 6 were waited for; matrix products, arithmetic and copies ran while one was open for 7% of the time, Pallas kernels for 0%

commit v1 on v0

--- a/solution.py
+++ b/solution.py
@@ -3,6 +3,18 @@
 import jax.numpy as jnp
 from jax import lax
 from jax.sharding import PartitionSpec as P
+
+
+def rotated_exchange(array, axis, split, join):
+    ways, here = (lax.axis_size(axis), lax.axis_index(axis))
+    width = array.shape[split] // ways
+    turned = jnp.roll(array, -here * width, axis=split)
+    got = [lax.slice_in_dim(turned, 0, width, axis=split)]
+    for far in range(1, ways):
+        sent = lax.slice_in_dim(turned, far * width, (far + 1) * width, axis=split)
+        got.append(lax.ppermute(sent, axis, [(d, (d + far) % ways) for d in range(ways)]))
+    line = jnp.concatenate(got[::-1], axis=join)
+    return jnp.roll(line, (here + 1) * got[0].shape[join], axis=join)
 
 
 def with_halo(x, sides, width):
@@ -156,7 +168,7 @@
     propa_padded = rimmed[2]
     screened = sandwich(screen_padded, polar_padded).astype(jnp.bfloat16)
     screen_owned, propa_owned = (
-        lax.all_to_all(screened, "energy", split_axis=4, concat_axis=0, tiled=True),
+        rotated_exchange(screened, "energy", 4, 0),
         lax.all_to_all(propa_masked, "energy", split_axis=4, concat_axis=0, tiled=True),
     )
     energy_count = screen_owned.shape[0]

time: 101 us -> 100 us (0.990)
  starting transfers between devices: 18.6 us -> 23 us
  waiting for transfers between devices: 25.1 us -> 21 us
    ppermute x0 -> x7, starting transfers between devices: none -> 6.35 us  [rotated_exchange(): lax.ppermute(sent, axis, [(d, (d + far) % ways) for d in range(ways)])]
    all_to_all x1 -> x0, waiting for transfers between devices: 5.9 us -> none  [local(): lax.all_to_all(screened, 'energy', split_axis=4, concat_axis=0, tiled=True)]
    ppermute x0 -> x7, waiting for transfers between devices: none -> 4.32 us  [rotated_exchange(): lax.ppermute(sent, axis, [(d, (d + far) % ways) for d in range(ways)])]
    all_to_all x1 -> x0, starting transfers between devices: 3.81 us -> none  [local(): lax.all_to_all(screened, 'energy', split_axis=4, concat_axis=0, tiled=True)]
    ppermute x2, waiting for transfers between devices: 9.03 us -> 7.05 us  [with_halo(): after = lax.ppermute(leading, axis, down)]
    ppermute x2, starting transfers between devices: 6.99 us -> 8.86 us  [with_halo(): before = lax.ppermute(last, axis, up)]
    another operation x2 -> x1, local copies, waits for them, and re-layouts: 1.93 us -> 0.77 us  [sandwich(): return jnp.stack(bands, axis=2)]
  transfers between devices with their start and end apart: 6 -> 12, of which waited for: 6 -> 9; matrix products, arithmetic and copies ran while one was open for 7% -> 6% of each run, Pallas kernels for 0% -> 0%
where the time goes in v1:
time: 100 us; the launch traced here: 99.7 us
  matrix products  34.4 us (34%)
  starting transfers between devices  23 us (23%)
  waiting for transfers between devices  21 us (21%)
  blocking collectives  10.8 us (11%)
  local copies, waits for them, and re-layouts  5.79 us (6%)
  other arithmetic  3.98 us (4%)
    dot_general x144, matrix products, product(): return jnp.einsum(form, lhs, rhs, preferred_element_type=jnp.float32)  23.9 us
    all_to_all x1, blocking collectives, local(): lax.all_to_all(sigma_owned, 'energy', split_axis=0, concat_axis=4, tiled=...  10.8 us
    dot_general x28, matrix products, plain_dot(): return jnp.dot(lhs, rhs, preferred_element_type=jnp.float32)  10.5 us
    ppermute x2, starting transfers between devices, with_halo(): before = lax.ppermute(last, axis, up)  8.86 us
    ppermute x2, waiting for transfers between devices, with_halo(): before = lax.ppermute(last, axis, up)  8.19 us
    ppermute x2, waiting for transfers between devices, with_halo(): after = lax.ppermute(leading, axis, down)  7.05 us
    ppermute x7, starting transfers between devices, rotated_exchange(): lax.ppermute(sent, axis, [(d, (d + far) % ways) for d in range(ways)])  6.35 us
    all_to_all x1, starting transfers between devices, local(): lax.all_to_all(propa_masked, 'energy', split_axis=4, concat_axis=0, tiled...  5.2 us
  transfers between devices with their start and end apart: 12, of which 9 were waited for; matrix products, arithmetic and copies ran while one was open for 6% of the time, Pallas kernels for 0%

profile of v1, /device:TPU:0, one launch (start us, length us, event | category | flops | bytes accessed | tf_op | source)
XLA Modules:
  0.0 99.7 jit_solution(11622258553412747567)
XLA Ops:
  0.1 1.4 %fusion.88 = (bf16[1,1,2,3,2,128,128]{6,5,2,4,3,1,0:T(8,128)(2,1)S(1)}, bf16[1,1,2,3,2,128,128]{6,5,2,4,3,1,0:T(8,128)(2,1)S(1)}, bf16[1,2,3,2,128,128]{5,4,1,3,2,0:T(8,128)(2,1)S(1)}) fusion(bf16[1,2,3,2,128,128]{5,4,3,2,1,0:T(8,128)(2,1)} %param.3, bf16[2,3]{0,1:T(4,128)(2,1)S(1)} %select_convert_fusion, bf16[1,2,3,2,128,128]{5,4,3,2,1,0:T(8,128)(2,1)} %param.4, ...), kind=kLoop, calls=%fused_computation.197 | loop fusion | flops 589824 | bytes 2359308 | tf_op jit(solution)/shard_map/stack | solution.py:165
  1.5 1.2 %copy.20 = bf16[1,2,3,2,128,128]{5,1,3,2,0,4:T(2,128)(2,1)} copy(bf16[1,2,3,2,128,128]{5,4,1,3,2,0:T(8,128)(2,1)S(1)} %get-tuple-element.66) | data formatting | bytes 786432 | tf_op jit(solution)/shard_map/mul | solution.py:41
  2.6 5.2 %all-to-all-start = ((bf16[1,2,3,2,128,128]{5,1,3,2,0,4:T(2,128)(2,1)}), bf16[1,2,3,2,128,128]{5,1,3,2,0,4:T(2,128)(2,1)S(1)}, u32[]{:S(2)}, u32[]{:S(2)}) async-start(bf16[1,2,3,2,128,128]{5,1,3,2,0,4:T(2,128)(2,1)} %copy.20), calls=%async_computation | async-start | bytes 786432 | tf_op jit(solution)/shard_map/all_to_all | solution.py:172
  8.0 1.2 %fusion.363 = (bf16[3,1,1,3,2,128,128]{6,5,2,4,3,1,0:T(8,128)(2,1)}, bf16[3,1,1,3,2,128,128]{6,5,2,4,3,1,0:T(8,128)(2,1)}) fusion(bf16[3,1,2,3,2,128,128]{6,5,2,4,3,1,0:T(8,128)(2,1)S(1)} %pad_maximum_fusion.1), kind=kLoop, calls=%fused_computation.620 | loop fusion | bytes 2359296 | tf_op jit(solution)/shard_map/slice | solution.py:25
  9.1 4.3 %collective-permute-start = (bf16[3,1,1,3,2,128,128]{6,5,2,4,3,1,0:T(8,128)(2,1)}, bf16[3,1,1,3,2,128,128]{6,5,2,4,3,1,0:T(8,128)(2,1)}, u32[]{:S(2)}, u32[]{:S(2)}) collective-permute-start(bf16[3,1,1,3,2,128,128]{6,5,2,4,3,1,0:T(8,128)(2,1)} %get-tuple-element.10), channel_id=1, source_target_pairs={{0,1},{1,2},{2,3},{4,5},{5,6},{6,7},{8,9},{9,10},{10,11},{12,13},{... | collective-permute-start | bytes 1769480 | tf_op jit(solution)/shard_map/ppermute | solution.py:27
  13.4 1.3 %collective-permute-start.1 = (bf16[3,1,1,3,2,128,128]{6,5,2,4,3,1,0:T(8,128)(2,1)}, bf16[3,1,1,3,2,128,128]{6,5,2,4,3,1,0:T(8,128)(2,1)}, u32[]{:S(2)}, u32[]{:S(2)}) collective-permute-start(bf16[3,1,1,3,2,128,128]{6,5,2,4,3,1,0:T(8,128)(2,1)} %get-tuple-element.11), channel_id=1, source_target_pairs={{1,0},{2,1},{3,2},{5,4},{6,5},{7,6},{9,8},{10,9},{11,10},{13,12},{... | collective-permute-start | bytes 1769480 | tf_op jit(solution)/shard_map/ppermute | solution.py:28
  14.7 1.4 %all-to-all-done = bf16[1,2,3,2,128,128]{5,1,3,2,0,4:T(2,128)(2,1)S(1)} async-done(((bf16[1,2,3,2,128,128]{5,1,3,2,0,4:T(2,128)(2,1)}), bf16[1,2,3,2,128,128]{5,1,3,2,0,4:T(2,128)(2,1)S(1)}, u32[]{:S(2)}, u32[]{:S(2)}) %all-to-all-start) | async-done | bytes 393248 | tf_op jit(solution)/shard_map/all_to_all | solution.py:172
  17.9 1.2 %fusion.3 = f32[16,12288]{1,0:T(8,128)} fusion(f32[16,12288]{1,0:T(8,128)S(1)} %convolution_add_fusion.7, f32[16,12288]{1,0:T(8,128)S(1)} %fusion.208, bf16[8,12288]{1,0:T(8,128)(2,1)S(1)} %reshape_squeeze.13), kind=kOutput, calls=%fused_computation.10 | convolution fusion | flops 3541248 | bytes 2555904 | tf_op jit(solution)/shard_map/dot_general | solution.py:105
  19.1 7.0 %collective-permute-done = bf16[3,1,1,3,2,128,128]{6,5,2,4,3,1,0:T(8,128)(2,1)} collective-permute-done((bf16[3,1,1,3,2,128,128]{6,5,2,4,3,1,0:T(8,128)(2,1)}, bf16[3,1,1,3,2,128,128]{6,5,2,4,3,1,0:T(8,128)(2,1)}, u32[]{:S(2)}, u32[]{:S(2)}) %collective-permute-start) | collective-permute-done | bytes 589856 | tf_op jit(solution)/shard_map/ppermute | solution.py:27
  26.2 4.9 %collective-permute-done.1 = bf16[3,1,1,3,2,128,128]{6,5,2,4,3,1,0:T(8,128)(2,1)} collective-permute-done((bf16[3,1,1,3,2,128,128]{6,5,2,4,3,1,0:T(8,128)(2,1)}, bf16[3,1,1,3,2,128,128]{6,5,2,4,3,1,0:T(8,128)(2,1)}, u32[]{:S(2)}, u32[]{:S(2)}) %collective-permute-start.1) | collective-permute-done | bytes 589856 | tf_op jit(solution)/shard_map/ppermute | solution.py:28
  31.1 1.4 %pad_maximum_fusion = bf16[3,1,4,3,2,128,128]{6,5,2,4,3,1,0:T(8,128)(2,1)S(1)} fusion(bf16[3,1,1,3,2,128,128]{6,5,2,4,3,1,0:T(8,128)(2,1)} %collective-permute-done.1, bf16[1,1,2,3,2,128,128]{6,5,2,4,3,1,0:T(8,128)(2,1)S(1)} %bitcast.724, bf16[1,1,2,3,2,128,128]{6,5,2,4,3,1,0:T(8,128)(2,1)S(1)} %get-tuple-element.65, ...), kind=kLoop, calls=%fused_computation.26 | loop fusion | flops 4718592 | bytes 4718592 | tf_op jit(solution)/shard_map/concatenate | solution.py:29
  45.8 1.2 %collective-permute-start.2 = (bf16[1,2,3,2,16,128]{5,4,1,3,2,0:T(8,128)(2,1)S(1)}, bf16[1,2,3,2,16,128]{5,4,1,3,2,0:T(8,128)(2,1)S(1)}, u32[]{:S(2)}, u32[]{:S(2)}) collective-permute-start(bf16[1,2,3,2,16,128]{5,4,1,3,2,0:T(8,128)(2,1)S(1)} %get-tuple-element.61), channel_id=1, source_target_pairs={{0,28},{4,0},{8,4},{12,8},{16,12},{20,16},{24,20},{28,24},{1,29},{... | collective-permute-start | bytes 147464 | tf_op jit(solution)/shard_map/ppermute | solution.py:15
  47.0 1.2 %fusion.204 = f32[16,12288]{1,0:T(8,128)} fusion(bf16[8,12288]{1,0:T(8,128)(2,1)S(1)} %reshape_squeeze.12), kind=kOutput, calls=%fused_computation.470 | convolution fusion | flops 3147648 | bytes 983040 | tf_op jit(solution)/shard_map/dot_general | solution.py:105
  48.2 1.4 %collective-permute-start.3 = (bf16[1,2,3,2,16,128]{5,4,1,3,2,0:T(8,128)(2,1)S(1)}, bf16[1,2,3,2,16,128]{5,4,1,3,2,0:T(8,128)(2,1)S(1)}, u32[]{:S(2)}, u32[]{:S(2)}) collective-permute-start(bf16[1,2,3,2,16,128]{5,4,1,3,2,0:T(8,128)(2,1)S(1)} %get-tuple-element.60), channel_id=1, source_target_pairs={{0,24},{4,28},{8,0},{12,4},{16,8},{20,12},{24,16},{28,20},{1,25},{... | collective-permute-start | bytes 147464 | tf_op jit(solution)/shard_map/ppermute | solution.py:15
  49.7 0.4 collective-permute-start.4
  50.0 1.5 %collective-permute-start.5 = (bf16[1,2,3,2,16,128]{5,4,1,3,2,0:T(8,128)(2,1)S(1)}, bf16[1,2,3,2,16,128]{5,4,1,3,2,0:T(8,128)(2,1)S(1)}, u32[]{:S(2)}, u32[]{:S(2)}) collective-permute-start(bf16[1,2,3,2,16,128]{5,4,1,3,2,0:T(8,128)(2,1)S(1)} %get-tuple-element.58), channel_id=1, source_target_pairs={{0,16},{4,20},{8,24},{12,28},{16,0},{20,4},{24,8},{28,12},{1,17},{... | collective-permute-start | bytes 147464 | tf_op jit(solution)/shard_map/ppermute | solution.py:15
  51.7 1.5 %collective-permute-start.7 = (bf16[1,2,3,2,16,128]{5,4,1,3,2,0:T(8,128)(2,1)S(1)}, bf16[1,2,3,2,16,128]{5,4,1,3,2,0:T(8,128)(2,1)S(1)}, u32[]{:S(2)}, u32[]{:S(2)}) collective-permute-start(bf16[1,2,3,2,16,128]{5,4,1,3,2,0:T(8,128)(2,1)S(1)} %get-tuple-element.56), channel_id=1, source_target_pairs={{0,8},{4,12},{8,16},{12,20},{16,24},{20,28},{24,0},{28,4},{1,9},{5... | collective-permute-start | bytes 147464 | tf_op jit(solution)/shard_map/ppermute | solution.py:15
  53.5 1.1 %collective-permute-done.5 = bf16[1,2,3,2,16,128]{5,4,1,3,2,0:T(8,128)(2,1)S(1)} collective-permute-done((bf16[1,2,3,2,16,128]{5,4,1,3,2,0:T(8,128)(2,1)S(1)}, bf16[1,2,3,2,16,128]{5,4,1,3,2,0:T(8,128)(2,1)S(1)}, u32[]{:S(2)}, u32[]{:S(2)}) %collective-permute-start.5) | collective-permute-done | bytes 49184 | tf_op jit(solution)/shard_map/ppermute | solution.py:15
  54.6 0.5 collective-permute-done.6
  55.1 2.1 %collective-permute-done.7 = bf16[1,2,3,2,16,128]{5,4,1,3,2,0:T(8,128)(2,1)S(1)} collective-permute-done((bf16[1,2,3,2,16,128]{5,4,1,3,2,0:T(8,128)(2,1)S(1)}, bf16[1,2,3,2,16,128]{5,4,1,3,2,0:T(8,128)(2,1)S(1)}, u32[]{:S(2)}, u32[]{:S(2)}) %collective-permute-start.7) | collective-permute-done | bytes 49184 | tf_op jit(solution)/shard_map/ppermute | solution.py:15
  57.2 0.6 collective-permute-done.8
  58.2 1.2 %fusion.206 = f32[16,12288]{1,0:T(8,128)} fusion(bf16[8,12288]{1,0:T(8,128)(2,1)S(1)} %reshape_squeeze.15), kind=kOutput, calls=%fused_computation.471 | convolution fusion | flops 3147648 | bytes 983040 | tf_op jit(solution)/shard_map/dot_general | solution.py:105
  60.4 0.3 convolution_add_fusion.5
  61.5 0.3 fusion
  61.8 0.5 copy-done.1
  62.6 0.4 multiply_subtract_fusion
  66.1 10.8 %all_to_all.36 = bf16[8,2,3,2,16,128]{5,4,2,1,3,0:T(8,128)(2,1)S(1)} all-to-all(bf16[8,2,3,2,16,128]{5,4,2,1,3,0:T(8,128)(2,1)S(1)} %pad_maximum_fusion.2), channel_id=1, replica_groups=mesh['energy'=8,'space'=4] {'energy'}, dimensions={0} | all-to-all | bytes 786432 | tf_op jit(solution)/shard_map/all_to_all | solution.py:177
  77.0 1.3 %collective-permute-start.10 = (bf16[1,1,3,2,128,128]{5,4,1,3,2,0:T(8,128)(2,1)S(1)}, bf16[1,1,3,2,128,128]{5,4,1,3,2,0:T(8,128)(2,1)S(1)}, u32[]{:S(2)}, u32[]{:S(2)}) collective-permute-start(bf16[1,1,3,2,128,128]{5,4,1,3,2,0:T(8,128)(2,1)S(1)} %get-tuple-element.54), channel_id=1, source_target_pairs={{1,0},{2,1},{3,2},{5,4},{6,5},{7,6},{9,8},{10,9},{11,10},{13,12},{... | collective-permute-start | bytes 589832 | tf_op jit(solution)/shard_map/ppermute | solution.py:28
  78.3 4.6 %collective-permute-start.9 = (bf16[1,1,3,2,128,128]{5,4,1,3,2,0:T(8,128)(2,1)S(1)}, bf16[1,1,3,2,128,128]{5,4,1,3,2,0:T(8,128)(2,1)S(1)}, u32[]{:S(2)}, u32[]{:S(2)}) collective-permute-start(bf16[1,1,3,2,128,128]{5,4,1,3,2,0:T(8,128)(2,1)S(1)} %get-tuple-element.53), channel_id=1, source_target_pairs={{0,1},{1,2},{2,3},{4,5},{5,6},{6,7},{8,9},{9,10},{10,11},{12,13},{... | collective-permute-start | bytes 589832 | tf_op jit(solution)/shard_map/ppermute | solution.py:27
  83.1 2.1 %collective-permute-done.10 = bf16[1,1,3,2,128,128]{5,4,1,3,2,0:T(8,128)(2,1)S(1)} collective-permute-done((bf16[1,1,3,2,128,128]{5,4,1,3,2,0:T(8,128)(2,1)S(1)}, bf16[1,1,3,2,128,128]{5,4,1,3,2,0:T(8,128)(2,1)S(1)}, u32[]{:S(2)}, u32[]{:S(2)}) %collective-permute-start.10) | collective-permute-done | bytes 196640 | tf_op jit(solution)/shard_map/ppermute | solution.py:28
  85.2 1.2 %collective-permute-done.9 = bf16[1,1,3,2,128,128]{5,4,1,3,2,0:T(8,128)(2,1)S(1)} collective-permute-done((bf16[1,1,3,2,128,128]{5,4,1,3,2,0:T(8,128)(2,1)S(1)}, bf16[1,1,3,2,128,128]{5,4,1,3,2,0:T(8,128)(2,1)S(1)}, u32[]{:S(2)}, u32[]{:S(2)}) %collective-permute-start.9) | collective-permute-done | bytes 196640 | tf_op jit(solution)/shard_map/ppermute | solution.py:27
  98.9 0.8 copy.27
  (230 shorter events, 33.5 us)
Async XLA Ops:
  2.6 13.5 %all-to-all-start = ((bf16[1,2,3,2,128,128]{5,1,3,2,0,4:T(2,128)(2,1)}), bf16[1,2,3,2,128,128]{5,1,3,2,0,4:T(2,128)(2,1)S(1)}, u32[]{:S(2)}, u32[]{:S(2)}) async-start(bf16[1,2,3,2,128,128]{5,1,3,2,0,4:T(2,128)(2,1)} %copy.20), calls=%async_computation | async-start | bytes 786432 | tf_op jit(solution)/shard_map/all_to_all | solution.py:172
  9.1 17.0 %collective-permute-start = (bf16[3,1,1,3,2,128,128]{6,5,2,4,3,1,0:T(8,128)(2,1)}, bf16[3,1,1,3,2,128,128]{6,5,2,4,3,1,0:T(8,128)(2,1)}, u32[]{:S(2)}, u32[]{:S(2)}) collective-permute-start(bf16[3,1,1,3,2,128,128]{6,5,2,4,3,1,0:T(8,128)(2,1)} %get-tuple-element.10), channel_id=1, source_target_pairs={{0,1},{1,2},{2,3},{4,5},{5,6},{6,7},{8,9},{9,10},{10,11},{12,13},{... | collective-permute-start | bytes 1769480 | tf_op jit(solution)/shard_map/ppermute | solution.py:27
  13.4 17.7 %collective-permute-start.1 = (bf16[3,1,1,3,2,128,128]{6,5,2,4,3,1,0:T(8,128)(2,1)}, bf16[3,1,1,3,2,128,128]{6,5,2,4,3,1,0:T(8,128)(2,1)}, u32[]{:S(2)}, u32[]{:S(2)}) collective-permute-start(bf16[3,1,1,3,2,128,128]{6,5,2,4,3,1,0:T(8,128)(2,1)} %get-tuple-element.11), channel_id=1, source_target_pairs={{1,0},{2,1},{3,2},{5,4},{6,5},{7,6},{9,8},{10,9},{11,10},{13,12},{... | collective-permute-start | bytes 1769480 | tf_op jit(solution)/shard_map/ppermute | solution.py:28
  45.8 5.9 %collective-permute-start.2 = (bf16[1,2,3,2,16,128]{5,4,1,3,2,0:T(8,128)(2,1)S(1)}, bf16[1,2,3,2,16,128]{5,4,1,3,2,0:T(8,128)(2,1)S(1)}, u32[]{:S(2)}, u32[]{:S(2)}) collective-permute-start(bf16[1,2,3,2,16,128]{5,4,1,3,2,0:T(8,128)(2,1)S(1)} %get-tuple-element.61), channel_id=1, source_target_pairs={{0,28},{4,0},{8,4},{12,8},{16,12},{20,16},{24,20},{28,24},{1,29},{... | collective-permute-start | bytes 147464 | tf_op jit(solution)/shard_map/ppermute | solution.py:15
  48.2 5.0 %collective-permute-start.3 = (bf16[1,2,3,2,16,128]{5,4,1,3,2,0:T(8,128)(2,1)S(1)}, bf16[1,2,3,2,16,128]{5,4,1,3,2,0:T(8,128)(2,1)S(1)}, u32[]{:S(2)}, u32[]{:S(2)}) collective-permute-start(bf16[1,2,3,2,16,128]{5,4,1,3,2,0:T(8,128)(2,1)S(1)} %get-tuple-element.60), channel_id=1, source_target_pairs={{0,24},{4,28},{8,0},{12,4},{16,8},{20,12},{24,16},{28,20},{1,25},{... | collective-permute-start | bytes 147464 | tf_op jit(solution)/shard_map/ppermute | solution.py:15
  49.7 3.8 %collective-permute-start.4 = (bf16[1,2,3,2,16,128]{5,4,1,3,2,0:T(8,128)(2,1)S(1)}, bf16[1,2,3,2,16,128]{5,4,1,3,2,0:T(8,128)(2,1)S(1)}, u32[]{:S(2)}, u32[]{:S(2)}) collective-permute-start(bf16[1,2,3,2,16,128]{5,4,1,3,2,0:T(8,128)(2,1)S(1)} %get-tuple-element.59), channel_id=1, source_target_pairs={{0,20},{4,24},{8,28},{12,0},{16,4},{20,8},{24,12},{28,16},{1,21},{... | collective-permute-start | bytes 147464 | tf_op jit(solution)/shard_map/ppermute | solution.py:15
  50.0 4.5 %collective-permute-start.5 = (bf16[1,2,3,2,16,128]{5,4,1,3,2,0:T(8,128)(2,1)S(1)}, bf16[1,2,3,2,16,128]{5,4,1,3,2,0:T(8,128)(2,1)S(1)}, u32[]{:S(2)}, u32[]{:S(2)}) collective-permute-start(bf16[1,2,3,2,16,128]{5,4,1,3,2,0:T(8,128)(2,1)S(1)} %get-tuple-element.58), channel_id=1, source_target_pairs={{0,16},{4,20},{8,24},{12,28},{16,0},{20,4},{24,8},{28,12},{1,17},{... | collective-permute-start | bytes 147464 | tf_op jit(solution)/shard_map/ppermute | solution.py:15
  51.5 3.6 %collective-permute-start.6 = (bf16[1,2,3,2,16,128]{5,4,1,3,2,0:T(8,128)(2,1)S(1)}, bf16[1,2,3,2,16,128]{5,4,1,3,2,0:T(8,128)(2,1)S(1)}, u32[]{:S(2)}, u32[]{:S(2)}) collective-permute-start(bf16[1,2,3,2,16,128]{5,4,1,3,2,0:T(8,128)(2,1)S(1)} %get-tuple-element.57), channel_id=1, source_target_pairs={{0,12},{4,16},{8,20},{12,24},{16,28},{20,0},{24,4},{28,8},{1,13},{... | collective-permute-start | bytes 147464 | tf_op jit(solution)/shard_map/ppermute | solution.py:15
  51.7 5.5 %collective-permute-start.7 = (bf16[1,2,3,2,16,128]{5,4,1,3,2,0:T(8,128)(2,1)S(1)}, bf16[1,2,3,2,16,128]{5,4,1,3,2,0:T(8,128)(2,1)S(1)}, u32[]{:S(2)}, u32[]{:S(2)}) collective-permute-start(bf16[1,2,3,2,16,128]{5,4,1,3,2,0:T(8,128)(2,1)S(1)} %get-tuple-element.56), channel_id=1, source_target_pairs={{0,8},{4,12},{8,16},{12,20},{16,24},{20,28},{24,0},{28,4},{1,9},{5... | collective-permute-start | bytes 147464 | tf_op jit(solution)/shard_map/ppermute | solution.py:15
  53.2 4.6 %collective-permute-start.8 = (bf16[1,2,3,2,16,128]{5,4,1,3,2,0:T(8,128)(2,1)S(1)}, bf16[1,2,3,2,16,128]{5,4,1,3,2,0:T(8,128)(2,1)S(1)}, u32[]{:S(2)}, u32[]{:S(2)}) collective-permute-start(bf16[1,2,3,2,16,128]{5,4,1,3,2,0:T(8,128)(2,1)S(1)} %get-tuple-element.55), channel_id=1, source_target_pairs={{0,4},{4,8},{8,12},{12,16},{16,20},{20,24},{24,28},{28,0},{1,5},{5... | collective-permute-start | bytes 147464 | tf_op jit(solution)/shard_map/ppermute | solution.py:15
  60.1 1.1 %copy-start = (f32[16,12288]{1,0:T(8,128)S(1)}, f32[16,12288]{1,0:T(8,128)}, u32[]{:S(2)}) copy-start(f32[16,12288]{1,0:T(8,128)} %fusion.206) | copy-start | bytes 2359300
  61.2 1.1 %copy-start.1 = (f32[16,12288]{1,0:T(8,128)S(1)}, f32[16,12288]{1,0:T(8,128)}, u32[]{:S(2)}) copy-start(f32[16,12288]{1,0:T(8,128)} %fusion.3) | copy-start | bytes 2359300
  61.2 1.4 %copy-start.2 = (f32[16,12288]{1,0:T(8,128)S(1)}, f32[16,12288]{1,0:T(8,128)}, u32[]{:S(2)}) copy-start(f32[16,12288]{1,0:T(8,128)} %fusion.204) | copy-start | bytes 2359300
  77.0 8.2 %collective-permute-start.10 = (bf16[1,1,3,2,128,128]{5,4,1,3,2,0:T(8,128)(2,1)S(1)}, bf16[1,1,3,2,128,128]{5,4,1,3,2,0:T(8,128)(2,1)S(1)}, u32[]{:S(2)}, u32[]{:S(2)}) collective-permute-start(bf16[1,1,3,2,128,128]{5,4,1,3,2,0:T(8,128)(2,1)S(1)} %get-tuple-element.54), channel_id=1, source_target_pairs={{1,0},{2,1},{3,2},{5,4},{6,5},{7,6},{9,8},{10,9},{11,10},{13,12},{... | collective-permute-start | bytes 589832 | tf_op jit(solution)/shard_map/ppermute | solution.py:28
  78.3 8.1 %collective-permute-start.9 = (bf16[1,1,3,2,128,128]{5,4,1,3,2,0:T(8,128)(2,1)S(1)}, bf16[1,1,3,2,128,128]{5,4,1,3,2,0:T(8,128)(2,1)S(1)}, u32[]{:S(2)}, u32[]{:S(2)}) collective-permute-start(bf16[1,1,3,2,128,128]{5,4,1,3,2,0:T(8,128)(2,1)S(1)} %get-tuple-element.53), channel_id=1, source_target_pairs={{0,1},{1,2},{2,3},{4,5},{5,6},{6,7},{8,9},{9,10},{10,11},{12,13},{... | collective-permute-start | bytes 589832 | tf_op jit(solution)/shard_map/ppermute | solution.py:27
